TPU v7x, 32 devices: a whole 2x2x4 slice. The times are simulated.
32 devices in a mesh: grp: 2 (over y), seq: 4 (over z), dp: 2 (over x), tp: 2 (over core).
Axes of the slice: x: 2, y: 2, z: 4, core: 2. Of those that a mesh axis runs over, the one named last changes fastest.
Arguments:
- query_image: bfloat16 [4, 1024, 2048], P(('grp', 'dp'), ('seq', 'tp')), parts along dimension 0, may hold values from -8 to 8
- key_image: bfloat16 [4, 1024, 2048], P(('grp', 'dp'), ('seq', 'tp')), parts along dimension 0, may hold values from -8 to 8
- value_image: bfloat16 [4, 1024, 2048], P(('grp', 'dp'), ('seq', 'tp')), parts along dimension 0, may hold values from -6 to 6
- query_text: bfloat16 [4, 128, 2048], P(('grp', 'dp'), ('seq', 'tp')), parts along dimension 0, may hold values from -6 to 6
- key_text: bfloat16 [4, 128, 2048], P(('grp', 'dp'), ('seq', 'tp')), parts along dimension 0, may hold values from -6 to 6
- value_text: bfloat16 [4, 128, 2048], P(('grp', 'dp'), ('seq', 'tp')), parts along dimension 0, may hold values from -6 to 6
- image_query_gain: float32 [128], replicated, may hold values from 1 to 6
- image_key_gain: float32 [128], replicated, may hold values from 1 to 6
- text_query_gain: float32 [128], replicated, may hold values from 1.2 to 2.5
- text_key_gain: float32 [128], replicated, may hold values from 1.2 to 2.5
- text_length: int32 [4], P(('grp', 'dp')), parts along dimension 0, may hold values from 1 to 128
- strata: int32 [4], P(('grp', 'dp')), parts along dimension 0, may hold values from 0 to 63
- image_state: bfloat16 [4, 1024, 3072], P(('grp', 'dp'), ('seq', 'tp')), parts along dimension 0, may hold values from -6 to 6
- target: bfloat16 [4, 1024, 3072], P(('grp', 'dp'), ('seq', 'tp')), parts along dimension 0, may hold values from -6 to 6
- out_weight: bfloat16 [2048, 3072], P('seq', 'tp'), may hold values from -0.125 to 0.125
- gate_table: bfloat16 [64, 3072], replicated, may hold values from -4 to 4
Outputs:
- velocity: bfloat16 [4, 1024, 3072], P(('grp', 'dp'), ('seq', 'tp')), parts along dimension 0
- text_attention: bfloat16 [4, 128, 2048], P(('grp', 'dp'), ('seq', 'tp')), parts along dimension 0
- flow_loss: float32 [2], P('grp'), parts along dimension 0
There are 2 independent parts, one for each index of `grp`. A program takes and returns all parts, laid end to end along the dimension named above; an argument that names none is the same for every part. Nothing has to cross between parts.
Inputs may be any that keep to these rules, and one draw needn't show every extreme that they name: `text_length`: text positions at or beyond a sample's length are padding and are not attended to.
All inputs are finite; a program needn't handle non-finite values.
Results may differ from a plain program's by a relative error of at most 0.012.
The roundings to bfloat16 on the way count: a program that leaves them out, or rounds other values in their place, can miss the bound.
Values may be sent and summed in bfloat16 or wider, within the bound.
A program may use at most 64 MiB of HBM per device.

v0:
```python
import jax
import jax.numpy as jnp
from jax import lax
from jax.sharding import PartitionSpec as P


def head_norm(values, gain_vector):
    head_dim = gain_vector.shape[0]
    columns = values.shape[-1]
    shaped = values.astype(jnp.float32).reshape(values.shape[:-1] + (columns // head_dim, head_dim))
    inverse = lax.rsqrt(jnp.mean(shaped * shaped, axis=-1, keepdims=True) + 1e-06)
    return (shaped * inverse * gain_vector).reshape(values.shape).astype(jnp.bfloat16)


def attend(query_block, key_split, value_split, usable, factor):
    scores = (
        jnp.einsum("qhd,khd->hqk", query_block, key_split, preferred_element_type=jnp.float32)
        * factor
    )
    scores = jnp.where(usable[None, None, :], scores, -1e30)
    row_max = jnp.max(scores, axis=2, keepdims=True)
    powers = jnp.exp(scores - row_max)
    weights = (powers / jnp.sum(powers, axis=2, keepdims=True)).astype(jnp.bfloat16)
    return jnp.einsum(
        "hqk,khd->qhd", weights, value_split, preferred_element_type=jnp.float32
    ).astype(jnp.bfloat16)


def local(
    query_image,
    key_image,
    value_image,
    query_text,
    key_text,
    value_text,
    image_query_gain,
    image_key_gain,
    text_query_gain,
    text_key_gain,
    text_length,
    strata,
    image_state,
    target,
    out_weight,
    gate_table,
):
    samples = query_image.shape[0]
    image_count = query_image.shape[1]
    text_count = query_text.shape[1]
    local_rows = image_count + text_count
    head_dim = image_query_gain.shape[0]
    seq_count = lax.axis_size("seq")
    core_count = lax.axis_size("tp")
    queries = jnp.concatenate(
        [head_norm(query_text, text_query_gain), head_norm(query_image, image_query_gain)], axis=1
    )
    keys_local = jnp.concatenate(
        [head_norm(key_text, text_key_gain), head_norm(key_image, image_key_gain)], axis=1
    )
    values_local = jnp.concatenate([value_text, value_image], axis=1)
    key_index = jnp.arange(seq_count * core_count * local_rows, dtype=jnp.int32)
    within = key_index % local_rows
    query_heads, key_rows, value_rows = (
        lax.all_to_all(queries, "seq", split_axis=2, concat_axis=1, tiled=True),
        lax.all_to_all(keys_local, "seq", split_axis=2, concat_axis=1, tiled=True),
        lax.all_to_all(values_local, "seq", split_axis=2, concat_axis=1, tiled=True),
    )
    key_heads, value_heads = (
        lax.all_gather(key_rows, "tp", axis=1, tiled=True),
        lax.all_gather(value_rows, "tp", axis=1, tiled=True),
    )
    core_shard = key_index // (seq_count * local_rows)
    seq_shard = key_index // local_rows % seq_count
    text_place = (seq_shard * core_count + core_shard) * text_count + within
    usable = (within[None, :] >= text_count) | (text_place[None, :] < text_length[:, None])
    query_total = query_heads.shape[1]
    heads_device = query_heads.shape[2] // head_dim
    block_rows = query_total // 4
    factor = head_dim ** (-0.5)

    def one_sample(operands):
        query_rows, key_sample, value_sample, usable_row = operands
        blocks = query_rows.reshape(4, block_rows, heads_device, head_dim)
        key_split = key_sample.reshape(key_sample.shape[0], heads_device, head_dim)
        value_split = value_sample.reshape(value_sample.shape[0], heads_device, head_dim)

        def one_block(block):
            return attend(block, key_split, value_split, usable_row, factor)

        outputs = lax.map(one_block, blocks)
        return outputs.reshape(query_total, heads_device * head_dim)

    head_output = lax.map(one_sample, (query_heads, key_heads, value_heads, usable))
    attention = lax.all_to_all(head_output, "seq", split_axis=1, concat_axis=2, tiled=True)
    text_attention = attention[:, :text_count]
    model_width = gate_table.shape[1]
    image_rows = attention[:, text_count:].reshape(samples * image_count, attention.shape[2])
    both_cores = lax.all_gather(image_rows, "tp", axis=0, tiled=True)
    half_columns = jnp.dot(
        both_cores,
        lax.all_gather(out_weight, "seq", axis=0, tiled=True),
        preferred_element_type=jnp.float32,
    )
    branch = lax.all_to_all(
        half_columns.astype(jnp.bfloat16), "tp", split_axis=0, concat_axis=1, tiled=True
    ).astype(half_columns.dtype)
    table_rows = gate_table.shape[0]
    selector = (strata[:, None] == jnp.arange(table_rows, dtype=jnp.int32)[None, :]).astype(
        jnp.bfloat16
    )
    gate_rows = jnp.dot(selector, gate_table, preferred_element_type=jnp.float32)
    combined = image_state.astype(jnp.float32) + gate_rows[:, None, :] * branch.reshape(
        samples, image_count, model_width
    )
    error_terms = combined - target.astype(jnp.float32)
    partial_sum = jnp.sum(error_terms * error_terms)
    total_sum = lax.psum(partial_sum, ("seq", "dp", "tp"))
    element_count = (
        samples * image_count * model_width * seq_count * core_count * lax.axis_size("dp")
    )
    flow_loss = (total_sum / element_count).reshape(1)
    return (combined.astype(jnp.bfloat16), text_attention, flow_loss)


def solution(mesh):
    placed = (
        P(("grp", "dp"), ("seq", "tp"), None),
        P(("grp", "dp"), ("seq", "tp"), None),
        P(("grp", "dp"), ("seq", "tp"), None),
        P(("grp", "dp"), ("seq", "tp"), None),
        P(("grp", "dp"), ("seq", "tp"), None),
        P(("grp", "dp"), ("seq", "tp"), None),
        P(),
        P(),
        P(),
        P(),
        P(("grp", "dp")),
        P(("grp", "dp")),
        P(("grp", "dp"), ("seq", "tp"), None),
        P(("grp", "dp"), ("seq", "tp"), None),
        P("seq", "tp"),
        P(),
    )
    return jax.shard_map(
        local,
        mesh=mesh,
        in_specs=placed,
        out_specs=(
            P(("grp", "dp"), ("seq", "tp"), None),
            P(("grp", "dp"), ("seq", "tp"), None),
            P("grp"),
        ),
        check_vma=False,
    )
```

profile of v0, /device:TPU:0, one launch (start us, length us, event | category | flops | bytes accessed | tf_op | source)
XLA Modules:
  0.0 360.4 jit_solution(4217201155704315449)
XLA Ops:
  12.9 11.6 %reduce.9 = bf16[2048,144]{1,0:T(8,128)(2,1)S(1)} reduce(bf16[2048,1,144]{2,1,0:T(2,128)(2,1)S(1)} %bitcast.85, bf16[]{:T(256)} %broadcast.226), dimensions={1}, to_apply=%bitcast.64.reduce_sub_computation | reduce | bytes 1179650
  24.6 2.3 reshape.298
  26.9 6.3 %all-to-all-start.1 = ((bf16[4,2,36864]{2,1,0:T(2,128)(2,1)}), bf16[4,2,36864]{2,1,0:T(2,128)(2,1)}, u32[]{:S(2)}, u32[]{:S(2)}) async-start(bf16[4,2,36864]{2,1,0:T(2,128)(2,1)} %reshape.298), calls=%async_computation.1 | async-start | bytes 1179648 | tf_op jit(solution)/shard_map/all_to_all | solution.py:65
  36.1 11.6 %reduce.10 = bf16[2048,144]{1,0:T(8,128)(2,1)S(1)} reduce(bf16[2048,1,144]{2,1,0:T(2,128)(2,1)S(1)} %bitcast.86, bf16[]{:T(256)} %broadcast.226), dimensions={1}, to_apply=%bitcast.66.reduce_sub_computation | reduce | bytes 1179650
  50.1 5.1 %all-to-all-start.2 = ((bf16[4,2,36864]{2,1,0:T(2,128)(2,1)}), bf16[4,2,36864]{2,1,0:T(2,128)(2,1)S(1)}, u32[]{:S(2)}, u32[]{:S(2)}) async-start(bf16[4,2,36864]{2,1,0:T(2,128)(2,1)} %reshape.300), calls=%async_computation.2 | async-start | bytes 1179648 | tf_op jit(solution)/shard_map/all_to_all | solution.py:66
  55.2 3.8 %reshape.299 = bf16[2048,1,144]{2,1,0:T(2,128)(2,1)S(1)} reshape(bf16[4,2,36864]{2,1,0:T(2,128)(2,1)} %all-to-all-done.1) | data formatting | bytes 1179648
  59.0 3.3 copy.126
  70.5 3.1 reshape.301
  73.6 3.3 copy.130
  81.6 11.6 %reduce.8 = bf16[2048,144]{1,0:T(8,128)(2,1)S(1)} reduce(bf16[2048,1,144]{2,1,0:T(2,128)(2,1)S(1)} %bitcast.89, bf16[]{:T(256)} %broadcast.226), dimensions={1}, to_apply=%bitcast.62.reduce_sub_computation | reduce | bytes 1179650
  93.2 2.3 reshape.296
  95.6 3.5 all-to-all-start
  99.1 15.4 %all-to-all-done = bf16[4,2,36864]{2,1,0:T(2,128)(2,1)S(1)} async-done(((bf16[4,2,36864]{2,1,0:T(2,128)(2,1)}), bf16[4,2,36864]{2,1,0:T(2,128)(2,1)S(1)}, u32[]{:S(2)}, u32[]{:S(2)}) %all-to-all-start) | async-done | bytes 589856 | tf_op jit(solution)/shard_map/all_to_all | solution.py:64
  114.5 3.1 reshape.297
  125.0 26.5 %while.18 = (s32[]{:T(128)}, bf16[4,144,4,128]{3,2,1,0:T(4,128)(2,1)}, bf16[4,144,4,128]{3,2,0,1:T(4,128)(2,1)S(1)}, bf16[1152,4,128]{2,0,1:T(8,128)(2,1)S(1)}, ...) while((s32[]{:T(128)}, bf16[4,144,4,128]{3,2,1,0:T(4,128)(2,1)}, ...), condition=%wide.region_7.8_spmd.clone, body=%wide.region_4.7_spmd.clone.sunk | while | flops 343836288 | bytes 8559957 | solution.py:90
  125.8 2.5 fusion.59
  128.3 2.7 fusion.60
  132.4 2.5 fusion.59
  134.9 2.7 fusion.60
  139.0 2.5 fusion.59
  141.5 2.7 fusion.60
  145.6 2.5 fusion.59
  148.1 2.7 fusion.60
  151.5 3.6 broadcast_in_dim.23
  155.1 4.2 %reduce.11 = bf16[576,512]{1,0:T(8,128)(2,1)S(1)} reduce(bf16[576,1,512]{2,1,0:T(2,128)(2,1)S(1)} %bitcast.91, bf16[]{:T(256)} %broadcast.226), dimensions={1}, to_apply=%bitcast.68.reduce_sub_computation | reduce | bytes 1179650
  159.8 17.8 %all_to_all.82 = bf16[4,2,36864]{2,1,0:T(2,128)(2,1)S(1)} all-to-all(bf16[4,2,36864]{2,1,0:T(2,128)(2,1)S(1)} %reshape.302), channel_id=1, replica_groups=mesh['grp'=2,'seq'=4,'dp'=2,'tp'=2] {'seq'}, dimensions={0} | all-to-all | bytes 1179648 | tf_op jit(solution)/shard_map/all_to_all | solution.py:94
  181.3 6.3 %all-gather.12.cloned.1.call-done = bf16[1,256,2048]{2,1,0:T(8,128)(2,1)} async-done(((bf16[1,128,2048]{2,1,0:T(8,128)(2,1)}), bf16[1,256,2048]{2,1,0:T(8,128)(2,1)}) %all-gather.12.cloned.1.call-update) | async-done | bytes 1048592 | tf_op jit(solution)/shard_map/all_gather | solution.py:98
  187.5 118.0 %all-gather.10.cloned.1.call-done = bf16[2048,1536]{1,0:T(8,128)(2,1)} async-done(((bf16[512,1536]{1,0:T(8,128)(2,1)}), bf16[2048,1536]{1,0:T(8,128)(2,1)}) %all-gather.10.cloned.1.call-update) | async-done | bytes 6291472 | tf_op jit(solution)/shard_map/all_gather | solution.py:101
  305.5 4.9 %convolution_convert_fusion = bf16[256,1536]{1,0:T(8,128)(2,1)S(1)} fusion(bf16[2048,1536]{1,0:T(8,128)(2,1)} %all-gather.10.cloned.1.call-done, bf16[1,256,2048]{2,1,0:T(8,128)(2,1)} %all-gather.12.cloned.1.call-done), kind=kOutput, calls=%fused_computation.42 | convolution fusion | flops 1611005952 | bytes 8126464 | tf_op jit(solution)/shard_map/dot_general | solution.py:99
  310.4 4.4 %all_to_all.83 = bf16[2,128,1536]{2,1,0:T(8,128)(2,1)S(1)} all-to-all(bf16[2,128,1536]{2,1,0:T(8,128)(2,1)S(1)} %bitcast.105), channel_id=1, replica_groups=mesh['grp'=2,'seq'=4,'dp'=2,'tp'=2] {'tp'}, dimensions={0} | all-to-all | bytes 1572864 | tf_op jit(solution)/shard_map/all_to_all | solution.py:104
  317.5 3.2 multiply_reduce_fusion
  320.8 31.3 %psum.7 = f32[]{:T(128)} all-reduce(f32[]{:T(128)} %get-tuple-element.125), channel_id=1, replica_groups=mesh['grp'=2,'seq'=4,'dp'=2,'tp'=2] {'seq','dp','tp'}, use_global_device_ids=true, to_apply=%region_9.10 | all-reduce | flops 1 | bytes 8 | tf_op jit(solution)/shard_map/psum | solution.py:117
  (116 shorter events, 42.9 us)
Async XLA Ops:
  7.2 173.3 %copy-start = (bf16[64,3072]{1,0:T(8,128)(2,1)S(1)}, bf16[64,3072]{1,0:T(8,128)(2,1)}, u32[]{:S(2)}) copy-start(bf16[64,3072]{1,0:T(8,128)(2,1)} %param.33) | copy-start | bytes 1179652
  9.1 0.7 copy-start.9
  9.1 0.8 copy-start.5
  9.5 0.8 copy-start.10
  9.5 1.1 copy-start.1
  24.5 8.7 %copy-start.2 = (bf16[1,128,2048]{2,1,0:T(8,128)(2,1)S(1)}, bf16[1,128,2048]{2,1,0:T(8,128)(2,1)}, u32[]{:S(2)}) copy-start(bf16[1,128,2048]{2,1,0:T(8,128)(2,1)} %param.18) | copy-start | bytes 1572868
  26.9 23.2 %all-to-all-start.1 = ((bf16[4,2,36864]{2,1,0:T(2,128)(2,1)}), bf16[4,2,36864]{2,1,0:T(2,128)(2,1)}, u32[]{:S(2)}, u32[]{:S(2)}) async-start(bf16[4,2,36864]{2,1,0:T(2,128)(2,1)} %reshape.298), calls=%async_computation.1 | async-start | bytes 1179648 | tf_op jit(solution)/shard_map/all_to_all | solution.py:65
  33.3 1.0 copy-start.4
  33.3 1.0 copy-start.8
  47.7 2.3 copy-start.6
  50.1 20.4 %all-to-all-start.2 = ((bf16[4,2,36864]{2,1,0:T(2,128)(2,1)}), bf16[4,2,36864]{2,1,0:T(2,128)(2,1)S(1)}, u32[]{:S(2)}, u32[]{:S(2)}) async-start(bf16[4,2,36864]{2,1,0:T(2,128)(2,1)} %reshape.300), calls=%async_computation.2 | async-start | bytes 1179648 | tf_op jit(solution)/shard_map/all_to_all | solution.py:66
  55.2 64.3 %all-gather.6.cloned.1.call-start = ((), (), s32[]{:S(2)}) async-start(), calls=%async_computation.5 | async-start | bytes 1769472 | tf_op jit(solution)/shard_map/all_gather | solution.py:69
  65.2 56.7 %all-gather.8.cloned.1.call-start = ((), (), s32[]{:S(2)}) async-start(), calls=%async_computation.6 | async-start | bytes 1769472 | tf_op jit(solution)/shard_map/all_gather | solution.py:70
  65.9 0.7 copy-start.11
  65.9 0.7 copy-start.12
  76.9 3.0 copy-start.7
  76.9 3.0 copy-start.3
  95.6 18.9 %all-to-all-start = ((bf16[4,2,36864]{2,1,0:T(2,128)(2,1)}), bf16[4,2,36864]{2,1,0:T(2,128)(2,1)S(1)}, u32[]{:S(2)}, u32[]{:S(2)}) async-start(bf16[4,2,36864]{2,1,0:T(2,128)(2,1)} %reshape.296), calls=%async_computation | async-start | bytes 1179648 | tf_op jit(solution)/shard_map/all_to_all | solution.py:64
  99.1 88.5 %all-gather.12.cloned.1.call-start = ((), (), s32[]{:S(2)}) async-start(), calls=%async_computation.8 | async-start | bytes 1572864 | tf_op jit(solution)/shard_map/all_gather | solution.py:98
  179.3 126.3 %all-gather.10.cloned.1.call-start = ((), (), s32[]{:S(2)}) async-start(), calls=%async_computation.7 | async-start | bytes 7864320 | tf_op jit(solution)/shard_map/all_gather | solution.py:101
Sparse Core Ops, SparseCore 0:
  65.4 10.6 all-gather.5
  80.0 8.7 all-gather.7
  179.4 8.1 all-gather.11
  189.0 116.4 all-gather.9
where the time goes:
time: 361 us; the launch traced here: 360 us
  waiting for transfers between devices  142 us (39%)
  local copies, waits for them, and re-layouts  57.3 us (16%)
  blocking collectives  53.5 us (15%)
  other arithmetic  49.7 us (14%)
  matrix products  25.7 us (7%)
  between operations  16.7 us (5%)
  starting transfers between devices  15.2 us (4%)
    all_gather x1, waiting for transfers between devices, local(): lax.all_gather(out_weight, 'seq', axis=0, tiled=True)  118 us
    unnamed x8, other arithmetic  40.4 us
    psum x1, blocking collectives, local(): total_sum = lax.psum(partial_sum, ('seq', 'dp', 'tp'))  31.3 us
    unnamed x42, local copies, waits for them, and re-layouts  22.5 us
    all_to_all x1, blocking collectives, local(): lax.all_to_all(head_output, 'seq', split_axis=1, concat_axis=2, tiled=True)  17.8 us
    all_to_all x1, waiting for transfers between devices, local(): lax.all_to_all(queries, 'seq', split_axis=2, concat_axis=1, tiled=True)  15.4 us
    dot_general x4, matrix products, attend(): jnp.einsum('hqk,khd->qhd', weights, value_split, preferred_element_type=j...  10.7 us
    sub x4, matrix products, attend(): powers = jnp.exp(scores - row_max)  9.95 us
  transfers between devices with their start and end apart: 7, of which 4 were waited for; matrix products, arithmetic and copies ran while one was open for 16% of the time, Pallas kernels for 0%

commit v1 on v0

--- a/solution.py
+++ b/solution.py
@@ -1,7 +1,16 @@
+import functools
+
 import jax
 import jax.numpy as jnp
 from jax import lax
+from jax.experimental import pallas as pl
+from jax.experimental.pallas import tpu as pltpu
 from jax.sharding import PartitionSpec as P
+
+MESH = pl.DeviceIdType.MESH
+VMEM = pl.BlockSpec(memory_space=pltpu.VMEM)
+ANY = pl.BlockSpec(memory_space=pl.ANY)
+SMALL = 1e-06
 
 
 def head_norm(values, gain_vector):
@@ -122,7 +131,384 @@
     return (combined.astype(jnp.bfloat16), text_attention, flow_loss)
 
 
+def norm_block(values, gains):
+    shaped = values.astype(jnp.float32)
+    inverse = lax.rsqrt(jnp.mean(shaped * shaped, axis=-1, keepdims=True) + SMALL)
+    return (shaped * inverse * gains).astype(jnp.bfloat16)
+
+
+def place(rank, cores):
+    return {"seq": rank // cores, "tp": rank % cores}
+
+
+def attend_kernel(
+    count, cores, factor,
+    qt, qi, kt, ki, vt, vi, gains, bias,
+    pair, text_out,
+    qb, kb, vb, ob, send, recv, osend, orecv, fsend, frecv,
+):
+    text, image = qt.shape[1], qi.shape[1]
+    rows = text + image
+    wide = qb.shape[1]
+    dim = gains.shape[1]
+    heads = wide // dim
+    core = lax.axis_index("tp")
+    me = lax.axis_index("seq") * cores + core
+    other = lax.rem(core + 1, cores)
+
+    barrier = pltpu.get_barrier_semaphore()
+    for o in range(1, count):
+        pl.semaphore_signal(
+            barrier, inc=1, device_id=place(lax.rem(me + o, count), cores), device_id_type=MESH
+        )
+    pl.semaphore_wait(barrier, count - 1)
+
+    def block(buffer, rank, start, size):
+        return buffer.at[pl.ds(pl.multiple_of(rank * rows + start, 16), size)]
+
+    def columns(rank):
+        return pl.ds(pl.multiple_of(rank * wide, wide), wide)
+
+    tensors = ((kt, ki, kb), (vt, vi, vb), (qt, qi, qb))
+
+    def inward(o, n):
+        peer = lax.rem(me + o, count)
+        out = []
+        for part, (source, start, size) in enumerate(
+            ((tensors[n][0], 0, text), (tensors[n][1], text, image))
+        ):
+            out.append((
+                source.at[0, :, columns(peer)],
+                block(tensors[n][2], me, start, size),
+                send.at[o, 2 * n + part],
+                recv.at[o, 2 * n + part],
+                peer,
+            ))
+        return out
+
+    def remote(args):
+        src, dst, s, r, peer = args
+        return pltpu.make_async_remote_copy(
+            src_ref=src, dst_ref=dst, send_sem=s, recv_sem=r,
+            device_id=place(peer, cores), device_id_type=MESH,
+        )
+
+    def near(args):
+        src, dst, s, r, peer = args
+        return pltpu.make_async_copy(src, dst, r)
+
+    for n in range(3):
+        for o in range(1, count):
+            for a in inward(o, n):
+                remote(a).start()
+        for a in inward(0, n):
+            near(a).start()
+
+    row = lax.broadcasted_iota(jnp.int32, (rows, dim), 0)
+    query_gain = jnp.where(row < text, gains[2:3, :], gains[0:1, :])
+    key_gain = jnp.where(row < text, gains[3:4, :], gains[1:2, :])
+
+    def take(buffer, rank, gain):
+        at = pl.ds(pl.multiple_of(rank * rows, 16), rows)
+        for h in range(heads):
+            cols = slice(h * dim, (h + 1) * dim)
+            buffer[at, cols] = norm_block(buffer[at, cols], gain)
+
+    def outward(o):
+        source = lax.rem(me - o + count, count)
+        home = source % cores
+        return [
+            (block(ob, source, 0, text), text_out.at[0, :, columns(me)],
+             osend.at[o, 0], orecv.at[o, 0], source),
+            (block(ob, source, text, image),
+             pair.at[pl.ds(pl.multiple_of(home * image, 16), image), columns(me)],
+             osend.at[o, 1], orecv.at[o, 1], source),
+        ]
+
+    def work(o):
+        source = lax.rem(me - o + count, count)
+        take(qb, source, query_gain)
+        at = pl.ds(pl.multiple_of(source * rows, 16), rows)
+        for h in range(heads):
+            cols = slice(h * dim, (h + 1) * dim)
+            scores = lax.dot_general(
+                qb[at, cols], kb[:, cols], (((1,), (1,)), ((), ())),
+                preferred_element_type=jnp.float32,
+            ) * factor + bias[...]
+            powers = jnp.exp(scores - jnp.max(scores, axis=1, keepdims=True))
+            scale = 1.0 / jnp.sum(powers, axis=1, keepdims=True)
+            weights = (powers * scale).astype(jnp.bfloat16)
+            ob[at, cols] = jnp.dot(
+                weights, vb[:, cols], preferred_element_type=jnp.float32
+            ).astype(jnp.bfloat16)
+
+    def wait_recv(o, n):
+        for a in inward(o, n):
+            remote(a).wait_recv()
+
+    for n in range(3):
+        for a in inward(0, n):
+            near(a).wait()
+    take(kb, me, key_gain)
+
+    def keys(o, carry):
+        wait_recv(o, 0)
+        take(kb, lax.rem(me - o + count, count), key_gain)
+        return carry
+
+    lax.fori_loop(1, count, keys, 0)
+
+    def values(o, carry):
+        wait_recv(o, 1)
+        return carry
+
+    lax.fori_loop(1, count, values, 0)
+
+    work(0)
+    for a in outward(0):
+        near(a).start()
+
+    def queries(o, carry):
+        wait_recv(o, 2)
+        work(o)
+        for a in outward(o):
+            remote(a).start()
+        return carry
+
+    lax.fori_loop(1, count, queries, 0)
+
+    def share(o):
+        sender = lax.rem(me + o, count)
+        mine = pl.ds(pl.multiple_of(core * image, 16), image)
+        return pltpu.make_async_remote_copy(
+            src_ref=pair.at[mine, columns(sender)], dst_ref=pair.at[mine, columns(sender)],
+            send_sem=fsend.at[o], recv_sem=frecv.at[o],
+            device_id={"tp": other}, device_id_type=MESH,
+        )
+
+    for a in outward(0):
+        near(a).wait()
+    share(0).start()
+
+    def homes(o, carry):
+        for a in outward(o):
+            remote(a).wait_recv()
+        share(o).start()
+        return carry
+
+    lax.fori_loop(1, count, homes, 0)
+
+    def ends(o, carry):
+        share(o).wait()
+        return carry
+
+    lax.fori_loop(0, count, ends, 0)
+
+    def drain(o, carry):
+        for n in range(3):
+            for a in inward(o, n):
+                remote(a).wait_send()
+        for a in outward(o):
+            remote(a).wait_send()
+        return carry
+
+    lax.fori_loop(1, count, drain, 0)
+
+
+def project_kernel(
+    sizes, tile,
+    pair, weight, state, target, gate,
+    velocity, loss,
+    acc, out, into, terms, send, recv, tsend, trecv,
+):
+    names = ("seq", "dp", "tp")
+    image = state.shape[1]
+    half = weight.shape[1]
+    where = [lax.axis_index(n) for n in names]
+    core = where[2]
+    other = lax.rem(core + 1, sizes[2])
+    total = sizes[0] * sizes[1] * sizes[2]
+    me = (where[0] * sizes[1] + where[1]) * sizes[2] + core
+
+    def device(rank):
+        return {
+            "seq": rank // (sizes[1] * sizes[2]),
+            "dp": rank // sizes[2] % sizes[1],
+            "tp": rank % sizes[2],
+        }
+
+    barrier = pltpu.get_barrier_semaphore()
+    for o in range(1, total):
+        pl.semaphore_signal(
+            barrier, inc=1, device_id=device(lax.rem(me + o, total)), device_id_type=MESH
+        )
+
+    theirs = pl.ds(pl.multiple_of(other * image, 16), image)
+    mine = pl.ds(pl.multiple_of(core * image, 16), image)
+    tiles = half // tile
+
+    def cross(j):
+        cols = slice(j * tile, (j + 1) * tile)
+        return pltpu.make_async_remote_copy(
+            src_ref=out.at[:, cols], dst_ref=into.at[:, cols],
+            send_sem=send.at[j], recv_sem=recv.at[j],
+            device_id={"tp": other}, device_id_type=MESH,
+        )
+
+    for j in range(tiles):
+        cols = slice(j * tile, (j + 1) * tile)
+        acc[:, cols] = jnp.dot(
+            pair[...], weight[:, cols], preferred_element_type=jnp.float32
+        )
+        out[:, cols] = acc[theirs, cols].astype(jnp.bfloat16)
+        if j == 0:
+            pl.semaphore_wait(barrier, total - 1)
+        cross(j).start()
+
+    def finish(branch, base, size):
+        cols = pl.ds(pl.multiple_of(base, 128), size)
+        combined = state[0, :, cols].astype(jnp.float32) + gate[:, cols] * branch
+        velocity[0, :, cols] = combined.astype(jnp.bfloat16)
+        error = combined - target[0, :, cols].astype(jnp.float32)
+        squares = error * error
+        lanes = squares[:, 0:128]
+        for k in range(1, size // 128):
+            lanes = lanes + squares[:, k * 128 : (k + 1) * 128]
+        return jnp.sum(lanes, axis=0, keepdims=True)
+
+    partial = jnp.zeros((1, 128), jnp.float32)
+    for j in range(tiles):
+        partial += finish(
+            acc[mine, j * tile : (j + 1) * tile], core * half + j * tile, tile
+        )
+    for j in range(tiles):
+        cross(j).wait_recv()
+        partial += finish(
+            into[:, j * tile : (j + 1) * tile].astype(jnp.float32), other * half + j * tile, tile
+        )
+    terms[0] = jnp.broadcast_to(partial, terms.shape[1:])
+
+    def tell(o):
+        return pltpu.make_async_remote_copy(
+            src_ref=terms.at[0], dst_ref=terms.at[o],
+            send_sem=tsend.at[o], recv_sem=trecv.at[o],
+            device_id=device(lax.rem(me + o, total)), device_id_type=MESH,
+        )
+
+    for o in range(1, total):
+        tell(o).start()
+    for j in range(tiles):
+        cross(j).wait_send()
+    for o in range(1, total):
+        tell(o).wait()
+    loss[...] = jnp.sum(terms[...], axis=0)
+
+
+def fast(
+    query_image,
+    key_image,
+    value_image,
+    query_text,
+    key_text,
+    value_text,
+    image_query_gain,
+    image_key_gain,
+    text_query_gain,
+    text_key_gain,
+    text_length,
+    strata,
+    image_state,
+    target,
+    out_weight,
+    gate_table,
+):
+    image = query_image.shape[1]
+    text = query_text.shape[1]
+    rows = image + text
+    attn = query_image.shape[2]
+    dim = image_query_gain.shape[0]
+    width = gate_table.shape[1]
+    seq, cores, dp, grp = (lax.axis_size(n) for n in ("seq", "tp", "dp", "grp"))
+    count = seq * cores
+    wide = attn // count
+    copies = grp * dp
+    piece = out_weight.shape[0] // copies
+    copy_index = lax.axis_index("grp") * dp + lax.axis_index("dp")
+    weight = lax.all_gather(
+        lax.dynamic_slice_in_dim(out_weight, copy_index * piece, piece, 0),
+        ("seq", "grp", "dp"), axis=0, tiled=True,
+    )
+    key_index = jnp.arange(count * rows, dtype=jnp.int32)
+    within = key_index % rows
+    usable = (within >= text) | (key_index // rows * text + within < text_length[0])
+    bias = jnp.where(usable, 0.0, -1e30).astype(jnp.float32)[None, :]
+    gains = jnp.stack([image_query_gain, image_key_gain, text_query_gain, text_key_gain])
+    table_rows = gate_table.shape[0]
+    selector = (strata[:, None] == jnp.arange(table_rows, dtype=jnp.int32)[None, :]).astype(
+        jnp.bfloat16
+    )
+    gate = jnp.dot(selector, gate_table, preferred_element_type=jnp.float32)
+    dma = pltpu.SemaphoreType.DMA
+    bf16 = jnp.bfloat16
+    pair, text_attention = pl.pallas_call(
+        functools.partial(attend_kernel, count, cores, dim ** (-0.5)),
+        out_shape=(
+            jax.ShapeDtypeStruct((cores * image, attn), bf16),
+            jax.ShapeDtypeStruct((1, text, attn), bf16),
+        ),
+        in_specs=[ANY] * 6 + [VMEM] * 2,
+        out_specs=(VMEM, VMEM),
+        scratch_shapes=[pltpu.VMEM((count * rows, wide), bf16)] * 4
+        + [dma((count, 6)), dma((count, 6)), dma((count, 2)), dma((count, 2)), dma((count,)), dma((count,))],
+        compiler_params=pltpu.CompilerParams(
+            collective_id=0, has_side_effects=True, vmem_limit_bytes=24 * 2**20
+        ),
+        cost_estimate=pl.CostEstimate(
+            flops=4 * count * rows * count * rows * wide,
+            bytes_accessed=200_000_000,
+            transcendentals=count * rows * count * rows,
+        ),
+    )(query_text, query_image, key_text, key_image, value_text, value_image, gains, bias)
+    half = width // cores
+    tile = half // 3 if half % 384 == 0 else half
+    sizes = (seq, dp, cores)
+    total = seq * dp * cores
+    velocity, loss = pl.pallas_call(
+        functools.partial(project_kernel, sizes, tile),
+        out_shape=(
+            jax.ShapeDtypeStruct((1, image, width), bf16),
+            jax.ShapeDtypeStruct((8, 128), jnp.float32),
+        ),
+        in_specs=[VMEM] * 5,
+        out_specs=(VMEM, VMEM),
+        scratch_shapes=[
+            pltpu.VMEM((cores * image, half), jnp.float32),
+            pltpu.VMEM((image, half), bf16),
+            pltpu.VMEM((image, half), bf16),
+            pltpu.VMEM((total, 8, 128), jnp.float32),
+            dma((half // tile,)), dma((half // tile,)), dma((total,)), dma((total,)),
+        ],
+        compiler_params=pltpu.CompilerParams(
+            collective_id=1, has_side_effects=True, vmem_limit_bytes=40 * 2**20
+        ),
+    )(pair, weight, image_state, target, gate)
+    flow_loss = (jnp.sum(loss[0]) / (image * width * total)).reshape(1)
+    return velocity, text_attention, flow_loss
+
+
 def solution(mesh):
+    def body(*operands):
+        samples, image, attn = operands[0].shape
+        heads = attn // operands[6].shape[0]
+        shape = dict(mesh.shape)
+        fits = (
+            samples == 1
+            and shape["tp"] == 2
+            and heads % (shape["seq"] * shape["tp"]) == 0
+            and operands[14].shape[0] % (16 * shape["grp"] * shape["dp"]) == 0
+        )
+        return fast(*operands) if fits else local(*operands)
+
     placed = (
         P(("grp", "dp"), ("seq", "tp"), None),
         P(("grp", "dp"), ("seq", "tp"), None),
@@ -142,7 +528,7 @@
         P(),
     )
     return jax.shard_map(
-        local,
+        body,
         mesh=mesh,
         in_specs=placed,
         out_specs=(

time: 361 us -> 165 us (0.46)
  waiting for transfers between devices: 142 us -> 33.1 us
  Pallas kernels: 0 us -> 97.1 us
  blocking collectives: 53.5 us -> 0 us
  other arithmetic: 49.7 us -> 1.34 us
  local copies, waits for them, and re-layouts: 57.3 us -> 15.3 us
  matrix products: 25.7 us -> 0.17 us
  starting transfers between devices: 15.2 us -> 0.04 us
    pallas_call x0 -> x2, Pallas kernels: none -> 97.1 us  [the longest x1 87.8 us: fast(): pl.pallas_call(functools.partial(attend_kernel, count, cores, dim ** (-0....]
    all_gather x4 -> x1, waiting for transfers between devices: 124 us -> 33.1 us  [fast(): lax.all_gather(lax.dynamic_slice_in_dim(out_weight, copy_index * piece, p...]
    unnamed x8 -> x0, other arithmetic: 40.4 us -> none
    psum x1 -> x0, blocking collectives: 31.3 us -> none  [local(): total_sum = lax.psum(partial_sum, ('seq', 'dp', 'tp'))]
    all_to_all x2 -> x0, blocking collectives: 22.2 us -> none  [the longest x1 17.8 us: local(): lax.all_to_all(head_output, 'seq', split_axis=1, concat_axis=2, tiled=True)]
    all_to_all x3 -> x0, waiting for transfers between devices: 17.3 us -> none  [the longest x1 15.4 us: local(): lax.all_to_all(queries, 'seq', split_axis=2, concat_axis=1, tiled=True)]
    dot_general x6 -> x1, matrix products: 15.8 us -> 0.17 us  [fast(): gate = jnp.dot(selector, gate_table, preferred_element_type=jnp.float32)]
    all_to_all x3 -> x0, starting transfers between devices: 14.9 us -> none  [the longest x1 6.35 us: local(): lax.all_to_all(keys_local, 'seq', split_axis=2, concat_axis=1, tiled=True)]
  transfers between devices with their start and end apart: 7 -> 1, of which waited for: 4 -> 1; matrix products, arithmetic and copies ran while one was open for 16% -> 1% of each run, Pallas kernels for 0% -> 53%
where the time goes in v1:
time: 165 us; the launch traced here: 164 us
  Pallas kernels  97.1 us (59%)
  waiting for transfers between devices  33.1 us (20%)
  between operations  17.2 us (10%)
  local copies, waits for them, and re-layouts  15.3 us (9%)
    pallas_call x1, Pallas kernels, fast(): pl.pallas_call(functools.partial(attend_kernel, count, cores, dim ** (-0....  87.8 us
    all_gather x1, waiting for transfers between devices, fast(): lax.all_gather(lax.dynamic_slice_in_dim(out_weight, copy_index * piece, p...  33.1 us
    unnamed x26, local copies, waits for them, and re-layouts  14.5 us
    pallas_call x1, Pallas kernels, fast(): pl.pallas_call(functools.partial(project_kernel, sizes, tile), out_shape=...  9.25 us
  transfers between devices with their start and end apart: 1, of which 1 were waited for; matrix products, arithmetic and copies ran while one was open for 1% of the time, Pallas kernels for 53%

profile of v1, /device:TPU:0, one launch (start us, length us, event | category | flops | bytes accessed | tf_op | source)
XLA Modules:
  0.0 164.2 jit_solution(4165992473671322674)
XLA Ops:
  7.2 0.0 copy-start
  7.2 0.0 all-gather.2.cloned.1.call-start
  7.2 1.3 copy-done
  8.6 0.8 constant_dynamic-slice_fusion
  9.3 0.0 all-gather.2.cloned.1.call-update
  10.7 0.7 pad_maximum_fusion.gains
  11.4 0.0 copy-start.5
  11.4 1.0 copy-done.5
  12.5 0.0 copy-start.6
  12.5 1.0 copy-done.6
  13.5 0.0 copy-start.7
  13.5 1.0 copy-done.7
  14.5 0.0 copy-start.8
  14.5 0.8 copy-done.8
  15.4 0.0 copy-start.9
  15.4 0.8 copy-done.9
  16.2 0.0 copy-start.10
  16.2 0.8 copy-done.10
  17.1 0.0 copy-start.11
  17.1 87.8 %shard_map.175 = (bf16[256,2048]{1,0:T(8,128)(2,1)S(1)}, bf16[1,16,2048]{2,1,0:T(8,128)(2,1)S(1)}) custom-call(bf16[1,16,2048]{2,1,0:T(8,128)(2,1)S(1)} %copy-done.8, bf16[1,128,2048]{2,1,0:T(8,128)(2,1)S(1)} %copy-done.5, bf16[1,16,2048]{2,1,0:T(8,128)(2,1)S(1)} %copy-done.9, bf16[1,128,2048]{2,1,0:T(8,128)(2,1)S(1)} %copy-done.6, ...), custom_call_target="tpu_custom_call" | custom-call | flops 1358954496 | bytes 200000000 | tf_op jit(solution)/shard_map/pallas_call | solution.py:453
  104.9 0.0 copy-done.11
  104.9 0.2 fusion.2.gate
  105.1 33.1 %all-gather.2.cloned.1.call-done.weight = bf16[2048,1536]{1,0:T(8,128)(2,1)} async-done(((bf16[128,1536]{1,0:T(8,128)(2,1)}), bf16[2048,1536]{1,0:T(8,128)(2,1)}) %all-gather.2.cloned.1.call-update) | async-done | bytes 6291472 | tf_op jit(solution)/shard_map/all_gather | solution.py:437
  138.2 0.0 copy-done.2
  138.2 2.8 %copy-done.1 = bf16[2048,1536]{1,0:T(8,128)(2,1)S(1)} copy-done((bf16[2048,1536]{1,0:T(8,128)(2,1)S(1)}, bf16[2048,1536]{1,0:T(8,128)(2,1)}, u32[]{:S(2)}) %copy-start.1) | copy-done | bytes 6291480
  141.0 1.1 copy-done.3
  142.1 9.3 %shard_map.176 = (bf16[1,128,3072]{2,1,0:T(8,128)(2,1)S(1)}, f32[8,128]{1,0:T(8,128)S(1)}) custom-call(bf16[256,2048]{1,0:T(8,128)(2,1)S(1)} %get-tuple-element.7.pair, bf16[2048,1536]{1,0:T(8,128)(2,1)S(1)} %copy-done.1, bf16[1,128,3072]{2,1,0:T(8,128)(2,1)S(1)} %copy-done.2, bf16[1,128,3072]{2,1,0:T(8,128)(2,1)S(1)} %copy-done.3, f32[1,3072]{1,0:T(1,128)S(1)} %fusion.2.gate), custom_call_target="tpu_custom_call" | custom-call | tf_op jit(solution)/shard_map/pallas_call | solution.py:476
  151.3 0.0 copy-start.4
  151.4 0.9 copy-done.4
  152.3 0.6 slice_reduce_fusion
  153.5 2.1 %copy.23 = bf16[1,128,3072]{2,1,0:T(8,128)(2,1)} copy(bf16[1,128,3072]{2,1,0:T(8,128)(2,1)} %copy-done.4) | data formatting | bytes 1572864
  155.6 0.6 copy.24
  (4 shorter events, 0.0 us)
Async XLA Ops:
  7.2 1.4 copy-start
  7.2 131.0 %all-gather.2.cloned.1.call-start = ((), (), s32[]{:S(2)}) async-start(), calls=%async_computation | async-start | bytes 6684672 | tf_op jit(solution)/shard_map/all_gather | solution.py:437
  11.4 1.0 copy-start.5
  12.5 1.0 copy-start.6
  13.5 1.0 copy-start.7
  14.5 0.8 copy-start.8
  15.4 0.8 copy-start.9
  16.2 0.8 copy-start.10
  17.1 87.9 %copy-start.11 = (bf16[64,3072]{1,0:T(8,128)(2,1)S(1)}, bf16[64,3072]{1,0:T(8,128)(2,1)}, u32[]{:S(2)}) copy-start(bf16[64,3072]{1,0:T(8,128)(2,1)} %param.31) | copy-start | bytes 1179652
  17.1 121.1 %copy-start.2 = (bf16[1,128,3072]{2,1,0:T(8,128)(2,1)S(1)}, bf16[1,128,3072]{2,1,0:T(8,128)(2,1)}, u32[]{:S(2)}) copy-start(bf16[1,128,3072]{2,1,0:T(8,128)(2,1)} %state.1) | copy-start | bytes 2359300
  138.2 2.8 %copy-start.1 = (bf16[2048,1536]{1,0:T(8,128)(2,1)S(1)}, bf16[2048,1536]{1,0:T(8,128)(2,1)}, u32[]{:S(2)}) copy-start(bf16[2048,1536]{1,0:T(8,128)(2,1)} %all-gather.2.cloned.1.call-done.weight) | copy-start | bytes 18874372
  141.0 1.1 copy-start.3
  151.3 0.9 copy-start.4
Sparse Core Ops, SparseCore 0:
  11.3 126.7 all-gather.1

commit v2 on v1

--- a/solution.py
+++ b/solution.py
@@ -2,6 +2,7 @@
 
 import jax
 import jax.numpy as jnp
+import numpy as np
 from jax import lax
 from jax.experimental import pallas as pl
 from jax.experimental.pallas import tpu as pltpu
@@ -137,31 +138,160 @@
     return (shaped * inverse * gains).astype(jnp.bfloat16)
 
 
-def place(rank, cores):
-    return {"seq": rank // cores, "tp": rank % cores}
-
-
-def attend_kernel(
-    count, cores, factor,
-    qt, qi, kt, ki, vt, vi, gains, bias,
-    pair, text_out,
-    qb, kb, vb, ob, send, recv, osend, orecv, fsend, frecv,
+def whole_kernel(
+    sizes, factor, tile,
+    qt, qi, kt, ki, vt, vi,
+    weight, state_in, target_in, table_in,
+    gain_qi, gain_ki, gain_qt, gain_kt, key_place, length, stratum,
+    velocity, text_out, loss,
+    qb, kb, vb, ob, pair, wb, state, target, table,
+    acc, out, into, terms,
+    send, recv, osend, orecv, fsend, frecv,
+    wsend, wrecv, xsend, xrecv, dsend, drecv,
+    lsem, psend, precv, tsend, trecv,
 ):
+    seq, dp, cores = sizes
+    count = seq * cores
+    total = seq * dp * cores
     text, image = qt.shape[1], qi.shape[1]
     rows = text + image
     wide = qb.shape[1]
-    dim = gains.shape[1]
+    dim = gain_qi.shape[1]
     heads = wide // dim
+    half = weight.shape[1]
+    z = lax.axis_index("seq")
+    x = lax.axis_index("dp")
+    y = lax.axis_index("grp")
     core = lax.axis_index("tp")
-    me = lax.axis_index("seq") * cores + core
+    me = z * cores + core
     other = lax.rem(core + 1, cores)
+    group = (z * dp + x) * cores + core
+
+    def place(rank):
+        return {"seq": rank // cores, "tp": rank % cores}
+
+    def member(rank):
+        return {
+            "seq": rank // (dp * cores),
+            "dp": rank // cores % dp,
+            "tp": rank % cores,
+        }
+
+    beside = ({"dp": 1 - x}, {"grp": 1 - y})
 
     barrier = pltpu.get_barrier_semaphore()
-    for o in range(1, count):
+    for o in range(1, total):
         pl.semaphore_signal(
-            barrier, inc=1, device_id=place(lax.rem(me + o, count), cores), device_id_type=MESH
-        )
-    pl.semaphore_wait(barrier, count - 1)
+            barrier, inc=1, device_id=member(lax.rem(group + o, total)), device_id_type=MESH
+        )
+    pl.semaphore_signal(barrier, inc=1, device_id=beside[1], device_id_type=MESH)
+
+    local_copies = [
+        pltpu.make_async_copy(
+            weight, wb.at[pl.ds(pl.multiple_of(z * weight.shape[0], 16), weight.shape[0])], lsem.at[0]
+        ),
+        pltpu.make_async_copy(state_in, state, lsem.at[1]),
+        pltpu.make_async_copy(target_in, target, lsem.at[2]),
+        pltpu.make_async_copy(table_in, table, lsem.at[3]),
+    ]
+
+    def remote(src, dst, s, r, device):
+        return pltpu.make_async_remote_copy(
+            src_ref=src, dst_ref=dst, send_sem=s, recv_sem=r,
+            device_id=device, device_id_type=MESH,
+        )
+
+    depth = weight.shape[0]
+    piece = depth // 4
+    quarter = y * 2 + x
+
+    def spot(block, q, start, size):
+        return wb.at[pl.ds(pl.multiple_of(block * depth + q * piece + start, 16), size)]
+
+    def hop(way, k):
+        step = 1 - 2 * way
+        origin = z - step * (k - 1)
+        source = (
+            weight.at[pl.ds(pl.multiple_of(quarter * piece, 16), piece)]
+            if k == 1 else spot(origin, quarter, 0, piece)
+        )
+        return remote(
+            source, spot(origin, quarter, 0, piece), wsend.at[way, k], wrecv.at[way, k],
+            {"seq": z + step},
+        )
+
+    def landed(way, k):
+        step = 1 - 2 * way
+        origin = z - step * k
+        ref = spot(origin, quarter, 0, piece)
+        return remote(ref, ref, wsend.at[way, k], wrecv.at[way, k], {"seq": z - step})
+
+    def has(way, k):
+        return z >= k if way == 0 else z < seq - k
+
+    def sends(way, k):
+        onward = z < seq - 1 if way == 0 else z > 0
+        return onward if k == 1 else jnp.logical_and(onward, has(way, k - 1))
+
+    def side(axis, way, k):
+        origin = z - (1 - 2 * way) * k
+        ref = spot(origin, quarter, 0, piece)
+        return remote(ref, ref, xsend.at[axis, way, k], xrecv.at[axis, way, k], beside[axis])
+
+    def side_quarter(axis):
+        return y * 2 + (1 - x) if axis == 0 else (1 - y) * 2 + x
+
+    def side_landed(axis, way, k):
+        origin = z - (1 - 2 * way) * k
+        ref = spot(origin, side_quarter(axis), 0, piece)
+        return remote(ref, ref, xsend.at[axis, way, k], xrecv.at[axis, way, k], beside[axis])
+
+    def corner(axis, way, k):
+        origin = z - (1 - 2 * way) * k
+        ref = spot(origin, side_quarter(axis), axis * (piece // 2), piece // 2)
+        return remote(
+            ref, ref, dsend.at[axis, way, k], drecv.at[axis, way, k], beside[1 - axis]
+        )
+
+    def corner_landed(axis, way, k):
+        origin = z - (1 - 2 * way) * k
+        ref = spot(origin, (1 - y) * 2 + (1 - x), axis * (piece // 2), piece // 2)
+        return remote(
+            ref, ref, dsend.at[axis, way, k], drecv.at[axis, way, k], beside[1 - axis]
+        )
+
+    def spread(k):
+        for way in range(2):
+            @pl.when(has(way, k))
+            def _():
+                landed(way, k).wait_recv()
+                if k + 1 < seq:
+                    @pl.when(sends(way, k + 1))
+                    def _():
+                        hop(way, k + 1).start()
+                side(0, way, k).start()
+                side(1, way, k).start()
+
+    def corners(k):
+        for way in range(2):
+            @pl.when(has(way, k))
+            def _():
+                for axis in range(2):
+                    side_landed(axis, way, k).wait_recv()
+                    corner(axis, way, k).start()
+
+    def settle(k):
+        for way in range(2):
+            @pl.when(sends(way, k))
+            def _():
+                hop(way, k).wait_send()
+
+            @pl.when(has(way, k))
+            def _():
+                for axis in range(2):
+                    side(axis, way, k).wait_send()
+                    corner(axis, way, k).wait_send()
+                    corner_landed(axis, way, k).wait_recv()
 
     def block(buffer, rank, start, size):
         return buffer.at[pl.ds(pl.multiple_of(rank * rows + start, 16), size)]
@@ -182,33 +312,22 @@
                 block(tensors[n][2], me, start, size),
                 send.at[o, 2 * n + part],
                 recv.at[o, 2 * n + part],
-                peer,
+                place(peer),
             ))
         return out
 
-    def remote(args):
-        src, dst, s, r, peer = args
-        return pltpu.make_async_remote_copy(
-            src_ref=src, dst_ref=dst, send_sem=s, recv_sem=r,
-            device_id=place(peer, cores), device_id_type=MESH,
-        )
-
     def near(args):
-        src, dst, s, r, peer = args
-        return pltpu.make_async_copy(src, dst, r)
-
-    for n in range(3):
+        return pltpu.make_async_copy(args[0], args[1], args[3])
+
+    def scatter(n):
         for o in range(1, count):
             for a in inward(o, n):
-                remote(a).start()
-        for a in inward(0, n):
-            near(a).start()
+                remote(*a).start()
 
     row = lax.broadcasted_iota(jnp.int32, (rows, dim), 0)
-    query_gain = jnp.where(row < text, gains[2:3, :], gains[0:1, :])
-    key_gain = jnp.where(row < text, gains[3:4, :], gains[1:2, :])
-
-    def take(buffer, rank, gain):
+
+    def take(buffer, rank, text_gain, image_gain):
+        gain = jnp.where(row < text, text_gain[...], image_gain[...])
         at = pl.ds(pl.multiple_of(rank * rows, 16), rows)
         for h in range(heads):
             cols = slice(h * dim, (h + 1) * dim)
@@ -219,22 +338,24 @@
         home = source % cores
         return [
             (block(ob, source, 0, text), text_out.at[0, :, columns(me)],
-             osend.at[o, 0], orecv.at[o, 0], source),
+             osend.at[o, 0], orecv.at[o, 0], place(source)),
             (block(ob, source, text, image),
              pair.at[pl.ds(pl.multiple_of(home * image, 16), image), columns(me)],
-             osend.at[o, 1], orecv.at[o, 1], source),
+             osend.at[o, 1], orecv.at[o, 1], place(source)),
         ]
+
+    bias = jnp.where(key_place[...] < length[0], 0.0, -1e30).astype(jnp.float32)
 
     def work(o):
         source = lax.rem(me - o + count, count)
-        take(qb, source, query_gain)
+        take(qb, source, gain_qt, gain_qi)
         at = pl.ds(pl.multiple_of(source * rows, 16), rows)
         for h in range(heads):
             cols = slice(h * dim, (h + 1) * dim)
             scores = lax.dot_general(
                 qb[at, cols], kb[:, cols], (((1,), (1,)), ((), ())),
                 preferred_element_type=jnp.float32,
-            ) * factor + bias[...]
+            ) * factor + bias
             powers = jnp.exp(scores - jnp.max(scores, axis=1, keepdims=True))
             scale = 1.0 / jnp.sum(powers, axis=1, keepdims=True)
             weights = (powers * scale).astype(jnp.bfloat16)
@@ -244,19 +365,38 @@
 
     def wait_recv(o, n):
         for a in inward(o, n):
-            remote(a).wait_recv()
-
+            remote(*a).wait_recv()
+
+    for n in range(3):
+        for a in inward(0, n):
+            near(a).start()
+    pl.semaphore_wait(barrier, total)
+    for way in range(2):
+        @pl.when(sends(way, 1))
+        def _():
+            hop(way, 1).start()
+    scatter(0)
+    for c in local_copies:
+        c.start()
     for n in range(3):
         for a in inward(0, n):
             near(a).wait()
-    take(kb, me, key_gain)
+    take(kb, me, gain_kt, gain_ki)
+    spread(1)
+    scatter(1)
 
     def keys(o, carry):
         wait_recv(o, 0)
-        take(kb, lax.rem(me - o + count, count), key_gain)
+        take(kb, lax.rem(me - o + count, count), gain_kt, gain_ki)
         return carry
 
+    if seq > 2:
+        spread(2)
+    scatter(2)
     lax.fori_loop(1, count, keys, 0)
+    for k in range(3, seq):
+        spread(k)
+    corners(1)
 
     def values(o, carry):
         wait_recv(o, 1)
@@ -267,107 +407,83 @@
     work(0)
     for a in outward(0):
         near(a).start()
+    for k in range(2, seq - 1):
+        corners(k)
 
     def queries(o, carry):
         wait_recv(o, 2)
         work(o)
         for a in outward(o):
-            remote(a).start()
+            remote(*a).start()
         return carry
 
     lax.fori_loop(1, count, queries, 0)
+    if seq > 2:
+        corners(seq - 1)
+
+    mine = pl.ds(pl.multiple_of(core * image, 16), image)
+    theirs = pl.ds(pl.multiple_of(other * image, 16), image)
 
     def share(o):
-        sender = lax.rem(me + o, count)
-        mine = pl.ds(pl.multiple_of(core * image, 16), image)
-        return pltpu.make_async_remote_copy(
-            src_ref=pair.at[mine, columns(sender)], dst_ref=pair.at[mine, columns(sender)],
-            send_sem=fsend.at[o], recv_sem=frecv.at[o],
-            device_id={"tp": other}, device_id_type=MESH,
-        )
+        ref = pair.at[mine, columns(lax.rem(me + o, count))]
+        return remote(ref, ref, fsend.at[o], frecv.at[o], {"tp": other})
+
+    def shared(o):
+        ref = pair.at[theirs, columns(lax.rem(z * cores + other + o, count))]
+        return remote(ref, ref, fsend.at[o], frecv.at[o], {"tp": other})
 
     for a in outward(0):
         near(a).wait()
     share(0).start()
+    for c in local_copies:
+        c.wait()
+    table_rows = table.shape[0]
+    selector = lax.broadcasted_iota(jnp.int32, (16, table_rows), 1) == stratum[0]
 
     def homes(o, carry):
         for a in outward(o):
-            remote(a).wait_recv()
+            src = a[0]
+            where = lax.rem(me + o, count)
+            dst = (
+                text_out.at[0, :, columns(where)]
+                if src.shape[0] == text
+                else pair.at[mine, columns(where)]
+            )
+            remote(dst, dst, a[2], a[3], a[4]).wait_recv()
         share(o).start()
         return carry
 
     lax.fori_loop(1, count, homes, 0)
 
     def ends(o, carry):
-        share(o).wait()
+        share(o).wait_send()
+        shared(o).wait_recv()
         return carry
 
     lax.fori_loop(0, count, ends, 0)
-
-    def drain(o, carry):
-        for n in range(3):
-            for a in inward(o, n):
-                remote(a).wait_send()
-        for a in outward(o):
-            remote(a).wait_send()
-        return carry
-
-    lax.fori_loop(1, count, drain, 0)
-
-
-def project_kernel(
-    sizes, tile,
-    pair, weight, state, target, gate,
-    velocity, loss,
-    acc, out, into, terms, send, recv, tsend, trecv,
-):
-    names = ("seq", "dp", "tp")
-    image = state.shape[1]
-    half = weight.shape[1]
-    where = [lax.axis_index(n) for n in names]
-    core = where[2]
-    other = lax.rem(core + 1, sizes[2])
-    total = sizes[0] * sizes[1] * sizes[2]
-    me = (where[0] * sizes[1] + where[1]) * sizes[2] + core
-
-    def device(rank):
-        return {
-            "seq": rank // (sizes[1] * sizes[2]),
-            "dp": rank // sizes[2] % sizes[1],
-            "tp": rank % sizes[2],
-        }
-
-    barrier = pltpu.get_barrier_semaphore()
-    for o in range(1, total):
-        pl.semaphore_signal(
-            barrier, inc=1, device_id=device(lax.rem(me + o, total)), device_id_type=MESH
-        )
-
-    theirs = pl.ds(pl.multiple_of(other * image, 16), image)
-    mine = pl.ds(pl.multiple_of(core * image, 16), image)
+    for k in range(1, seq):
+        settle(k)
+
     tiles = half // tile
 
     def cross(j):
         cols = slice(j * tile, (j + 1) * tile)
-        return pltpu.make_async_remote_copy(
-            src_ref=out.at[:, cols], dst_ref=into.at[:, cols],
-            send_sem=send.at[j], recv_sem=recv.at[j],
-            device_id={"tp": other}, device_id_type=MESH,
+        return remote(
+            out.at[:, cols], into.at[:, cols], psend.at[j], precv.at[j], {"tp": other}
         )
 
     for j in range(tiles):
         cols = slice(j * tile, (j + 1) * tile)
-        acc[:, cols] = jnp.dot(
-            pair[...], weight[:, cols], preferred_element_type=jnp.float32
-        )
+        acc[:, cols] = jnp.dot(pair[...], wb[:, cols], preferred_element_type=jnp.float32)
         out[:, cols] = acc[theirs, cols].astype(jnp.bfloat16)
-        if j == 0:
-            pl.semaphore_wait(barrier, total - 1)
         cross(j).start()
 
     def finish(branch, base, size):
         cols = pl.ds(pl.multiple_of(base, 128), size)
-        combined = state[0, :, cols].astype(jnp.float32) + gate[:, cols] * branch
+        gate = jnp.dot(
+            selector.astype(jnp.bfloat16), table[:, cols], preferred_element_type=jnp.float32
+        )[0:1]
+        combined = state[0, :, cols].astype(jnp.float32) + gate * branch
         velocity[0, :, cols] = combined.astype(jnp.bfloat16)
         error = combined - target[0, :, cols].astype(jnp.float32)
         squares = error * error
@@ -389,19 +505,29 @@
     terms[0] = jnp.broadcast_to(partial, terms.shape[1:])
 
     def tell(o):
-        return pltpu.make_async_remote_copy(
-            src_ref=terms.at[0], dst_ref=terms.at[o],
-            send_sem=tsend.at[o], recv_sem=trecv.at[o],
-            device_id=device(lax.rem(me + o, total)), device_id_type=MESH,
+        return remote(
+            terms.at[0], terms.at[o], tsend.at[o], trecv.at[o],
+            member(lax.rem(group + o, total)),
         )
 
     for o in range(1, total):
         tell(o).start()
     for j in range(tiles):
         cross(j).wait_send()
+
+    def drain(o, carry):
+        for n in range(3):
+            for a in inward(o, n):
+                remote(*a).wait_send()
+        for a in outward(o):
+            remote(*a).wait_send()
+        return carry
+
+    lax.fori_loop(1, count, drain, 0)
     for o in range(1, total):
         tell(o).wait()
-    loss[...] = jnp.sum(terms[...], axis=0)
+    whole = jnp.sum(jnp.sum(terms[...], axis=0)[0:1])
+    loss[0] = whole / (image * velocity.shape[2] * total)
 
 
 def fast(
@@ -428,72 +554,54 @@
     attn = query_image.shape[2]
     dim = image_query_gain.shape[0]
     width = gate_table.shape[1]
-    seq, cores, dp, grp = (lax.axis_size(n) for n in ("seq", "tp", "dp", "grp"))
+    seq, cores, dp = (lax.axis_size(n) for n in ("seq", "tp", "dp"))
+    sizes = (seq, dp, cores)
     count = seq * cores
+    total = seq * dp * cores
     wide = attn // count
-    copies = grp * dp
-    piece = out_weight.shape[0] // copies
-    copy_index = lax.axis_index("grp") * dp + lax.axis_index("dp")
-    weight = lax.all_gather(
-        lax.dynamic_slice_in_dim(out_weight, copy_index * piece, piece, 0),
-        ("seq", "grp", "dp"), axis=0, tiled=True,
-    )
-    key_index = jnp.arange(count * rows, dtype=jnp.int32)
+    half = width // cores
+    tile = half // 3 if half % 384 == 0 else half
+    key_index = np.arange(count * rows, dtype=np.int32)
     within = key_index % rows
-    usable = (within >= text) | (key_index // rows * text + within < text_length[0])
-    bias = jnp.where(usable, 0.0, -1e30).astype(jnp.float32)[None, :]
-    gains = jnp.stack([image_query_gain, image_key_gain, text_query_gain, text_key_gain])
-    table_rows = gate_table.shape[0]
-    selector = (strata[:, None] == jnp.arange(table_rows, dtype=jnp.int32)[None, :]).astype(
-        jnp.bfloat16
-    )
-    gate = jnp.dot(selector, gate_table, preferred_element_type=jnp.float32)
+    key_place = np.where(within < text, key_index // rows * text + within, -1)[None, :]
     dma = pltpu.SemaphoreType.DMA
     bf16 = jnp.bfloat16
-    pair, text_attention = pl.pallas_call(
-        functools.partial(attend_kernel, count, cores, dim ** (-0.5)),
-        out_shape=(
-            jax.ShapeDtypeStruct((cores * image, attn), bf16),
-            jax.ShapeDtypeStruct((1, text, attn), bf16),
-        ),
-        in_specs=[ANY] * 6 + [VMEM] * 2,
-        out_specs=(VMEM, VMEM),
-        scratch_shapes=[pltpu.VMEM((count * rows, wide), bf16)] * 4
-        + [dma((count, 6)), dma((count, 6)), dma((count, 2)), dma((count, 2)), dma((count,)), dma((count,))],
-        compiler_params=pltpu.CompilerParams(
-            collective_id=0, has_side_effects=True, vmem_limit_bytes=24 * 2**20
-        ),
-        cost_estimate=pl.CostEstimate(
-            flops=4 * count * rows * count * rows * wide,
-            bytes_accessed=200_000_000,
-            transcendentals=count * rows * count * rows,
-        ),
-    )(query_text, query_image, key_text, key_image, value_text, value_image, gains, bias)
-    half = width // cores
-    tile = half // 3 if half % 384 == 0 else half
-    sizes = (seq, dp, cores)
-    total = seq * dp * cores
-    velocity, loss = pl.pallas_call(
-        functools.partial(project_kernel, sizes, tile),
+    smem = pl.BlockSpec(memory_space=pltpu.SMEM)
+    return pl.pallas_call(
+        functools.partial(whole_kernel, sizes, dim ** (-0.5), tile),
         out_shape=(
             jax.ShapeDtypeStruct((1, image, width), bf16),
-            jax.ShapeDtypeStruct((8, 128), jnp.float32),
+            jax.ShapeDtypeStruct((1, text, attn), bf16),
+            jax.ShapeDtypeStruct((1,), jnp.float32),
         ),
-        in_specs=[VMEM] * 5,
-        out_specs=(VMEM, VMEM),
-        scratch_shapes=[
+        in_specs=[ANY] * 10 + [VMEM] * 5 + [smem] * 2,
+        out_specs=(VMEM, VMEM, smem),
+        scratch_shapes=[pltpu.VMEM((count * rows, wide), bf16)] * 4
+        + [
+            pltpu.VMEM((cores * image, attn), bf16),
+            pltpu.VMEM((attn, half), bf16),
+            pltpu.VMEM((1, image, width), bf16),
+            pltpu.VMEM((1, image, width), bf16),
+            pltpu.VMEM(gate_table.shape, bf16),
             pltpu.VMEM((cores * image, half), jnp.float32),
             pltpu.VMEM((image, half), bf16),
             pltpu.VMEM((image, half), bf16),
             pltpu.VMEM((total, 8, 128), jnp.float32),
-            dma((half // tile,)), dma((half // tile,)), dma((total,)), dma((total,)),
+            dma((count, 6)), dma((count, 6)), dma((count, 2)), dma((count, 2)),
+            dma((count,)), dma((count,)),
+            dma((2, seq)), dma((2, seq)), dma((2, 2, seq)), dma((2, 2, seq)),
+            dma((2, 2, seq)), dma((2, 2, seq)),
+            dma((4,)), dma((half // tile,)), dma((half // tile,)), dma((total,)), dma((total,)),
         ],
         compiler_params=pltpu.CompilerParams(
-            collective_id=1, has_side_effects=True, vmem_limit_bytes=40 * 2**20
+            collective_id=0, has_side_effects=True, vmem_limit_bytes=60 * 2**20
         ),
-    )(pair, weight, image_state, target, gate)
-    flow_loss = (jnp.sum(loss[0]) / (image * width * total)).reshape(1)
-    return velocity, text_attention, flow_loss
+    )(
+        query_text, query_image, key_text, key_image, value_text, value_image,
+        out_weight, image_state, target, gate_table,
+        image_query_gain[None], image_key_gain[None], text_query_gain[None], text_key_gain[None],
+        jnp.asarray(key_place, jnp.int32), text_length, strata,
+    )
 
 
 def solution(mesh):
@@ -505,7 +613,9 @@
             samples == 1
             and shape["tp"] == 2
             and heads % (shape["seq"] * shape["tp"]) == 0
-            and operands[14].shape[0] % (16 * shape["grp"] * shape["dp"]) == 0
+            and shape["grp"] == 2
+            and shape["dp"] == 2
+            and operands[14].shape[0] % 128 == 0
         )
         return fast(*operands) if fits else local(*operands)
 

time: 165 us -> 105 us (0.64)
  waiting for transfers between devices: 33.1 us -> 0 us
  between operations: 17.2 us -> 3.63 us
  local copies, waits for them, and re-layouts: 15.3 us -> 2.73 us
    all_gather x1 -> x0, waiting for transfers between devices: 33.1 us -> none  [fast(): lax.all_gather(lax.dynamic_slice_in_dim(out_weight, copy_index * piece, p...]
    unnamed x26 -> x4, local copies, waits for them, and re-layouts: 14.5 us -> 2.73 us
    pallas_call x2 -> x1, Pallas kernels: 97.1 us -> 98 us  [fast(): pl.pallas_call(functools.partial(whole_kernel, sizes, dim ** (-0.5), tile...]
  transfers between devices with their start and end apart: 1 -> 0, of which waited for: 1 -> 0; matrix products, arithmetic and copies ran while one was open for 1% -> 0% of each run, Pallas kernels for 53% -> 0%
where the time goes in v2:
time: 105 us; the launch traced here: 104 us
  Pallas kernels  98 us (93%)
  between operations  3.63 us (3%)
  local copies, waits for them, and re-layouts  2.73 us (3%)
    pallas_call x1, Pallas kernels, fast(): pl.pallas_call(functools.partial(whole_kernel, sizes, dim ** (-0.5), tile...  98 us
    unnamed x4, local copies, waits for them, and re-layouts  2.73 us

profile of v2, /device:TPU:0, one launch (start us, length us, event | category | flops | bytes accessed | tf_op | source)
XLA Modules:
  0.0 104.3 jit_solution(2274632004373398639)
XLA Ops:
  1.9 98.0 %shard_map.184 = (bf16[1,128,3072]{2,1,0:T(8,128)(2,1)}, bf16[1,16,2048]{2,1,0:T(8,128)(2,1)}, f32[1]{0:T(128)}) custom-call(bf16[1,16,2048]{2,1,0:T(8,128)(2,1)} %qt.1, bf16[1,128,2048]{2,1,0:T(8,128)(2,1)} %qi.1, bf16[1,16,2048]{2,1,0:T(8,128)(2,1)} %kt.1, bf16[1,128,2048]{2,1,0:T(8,128)(2,1)} %ki.1, bf16[1,16,2048]{2,1,0:T(8,128)(2,1)} %vt.1, ...), custom_call_target="tpu_custom_call" | custom-call | tf_op jit(solution)/shard_map/pallas_call | solution.py:570
  99.9 0.0 copy-start
  99.9 2.1 %copy.25 = bf16[1,128,3072]{2,1,0:T(8,128)(2,1)} copy(bf16[1,128,3072]{2,1,0:T(8,128)(2,1)} %get-tuple-element.6) | data formatting | bytes 1572864
  102.0 0.0 copy-done
  102.0 0.6 copy.26
Async XLA Ops:
  99.9 2.1 %copy-start = (bf16[1,16,2048]{2,1,0:T(8,128)(2,1)S(1)}, bf16[1,16,2048]{2,1,0:T(8,128)(2,1)}, u32[]{:S(2)}) copy-start(bf16[1,16,2048]{2,1,0:T(8,128)(2,1)} %get-tuple-element.7) | copy-start | bytes 196612

commit v3 on v2

--- a/solution.py
+++ b/solution.py
@@ -143,8 +143,8 @@
     qt, qi, kt, ki, vt, vi,
     weight, state_in, target_in, table_in,
     gain_qi, gain_ki, gain_qt, gain_kt, key_place, length, stratum,
-    velocity, text_out, loss,
-    qb, kb, vb, ob, pair, wb, state, target, table,
+    velocity_out, text_out, loss,
+    velocity, qb, kb, vb, ob, pair, wb, state, target, table,
     acc, out, into, terms,
     send, recv, osend, orecv, fsend, frecv,
     wsend, wrecv, xsend, xrecv, dsend, drecv,
@@ -167,6 +167,18 @@
     other = lax.rem(core + 1, cores)
     group = (z * dp + x) * cores + core
 
+    def ahead(o):
+        return lax.rem(z + o // cores, seq) * cores + lax.rem(core + o % cores, cores)
+
+    def behind(o):
+        return (
+            lax.rem(z - o // cores + seq, seq) * cores
+            + lax.rem(core - o % cores + cores, cores)
+        )
+
+    def turn(i):
+        return i
+
     def place(rank):
         return {"seq": rank // cores, "tp": rank % cores}
 
@@ -302,7 +314,7 @@
     tensors = ((kt, ki, kb), (vt, vi, vb), (qt, qi, qb))
 
     def inward(o, n):
-        peer = lax.rem(me + o, count)
+        peer = ahead(o)
         out = []
         for part, (source, start, size) in enumerate(
             ((tensors[n][0], 0, text), (tensors[n][1], text, image))
@@ -320,8 +332,8 @@
         return pltpu.make_async_copy(args[0], args[1], args[3])
 
     def scatter(n):
-        for o in range(1, count):
-            for a in inward(o, n):
+        for i in range(1, count):
+            for a in inward(turn(i), n):
                 remote(*a).start()
 
     row = lax.broadcasted_iota(jnp.int32, (rows, dim), 0)
@@ -334,7 +346,7 @@
             buffer[at, cols] = norm_block(buffer[at, cols], gain)
 
     def outward(o):
-        source = lax.rem(me - o + count, count)
+        source = behind(o)
         home = source % cores
         return [
             (block(ob, source, 0, text), text_out.at[0, :, columns(me)],
@@ -347,7 +359,7 @@
     bias = jnp.where(key_place[...] < length[0], 0.0, -1e30).astype(jnp.float32)
 
     def work(o):
-        source = lax.rem(me - o + count, count)
+        source = behind(o)
         take(qb, source, gain_qt, gain_qi)
         at = pl.ds(pl.multiple_of(source * rows, 16), rows)
         for h in range(heads):
@@ -385,32 +397,34 @@
     spread(1)
     scatter(1)
 
-    def keys(o, carry):
+    def keys(i, carry):
+        o = turn(i)
         wait_recv(o, 0)
-        take(kb, lax.rem(me - o + count, count), gain_kt, gain_ki)
+        take(kb, behind(o), gain_kt, gain_ki)
         return carry
 
     if seq > 2:
         spread(2)
     scatter(2)
     lax.fori_loop(1, count, keys, 0)
+
+    def values(o, carry):
+        wait_recv(o, 1)
+        return carry
+
+    lax.fori_loop(1, count, values, 0)
+
     for k in range(3, seq):
         spread(k)
     corners(1)
-
-    def values(o, carry):
-        wait_recv(o, 1)
-        return carry
-
-    lax.fori_loop(1, count, values, 0)
-
     work(0)
     for a in outward(0):
         near(a).start()
     for k in range(2, seq - 1):
         corners(k)
 
-    def queries(o, carry):
+    def queries(i, carry):
+        o = turn(i)
         wait_recv(o, 2)
         work(o)
         for a in outward(o):
@@ -425,11 +439,13 @@
     theirs = pl.ds(pl.multiple_of(other * image, 16), image)
 
     def share(o):
-        ref = pair.at[mine, columns(lax.rem(me + o, count))]
+        ref = pair.at[mine, columns(ahead(o))]
         return remote(ref, ref, fsend.at[o], frecv.at[o], {"tp": other})
 
     def shared(o):
-        ref = pair.at[theirs, columns(lax.rem(z * cores + other + o, count))]
+        ref = pair.at[theirs, columns(
+            lax.rem(z + o // cores, seq) * cores + lax.rem(other + o % cores, cores)
+        )]
         return remote(ref, ref, fsend.at[o], frecv.at[o], {"tp": other})
 
     for a in outward(0):
@@ -440,10 +456,11 @@
     table_rows = table.shape[0]
     selector = lax.broadcasted_iota(jnp.int32, (16, table_rows), 1) == stratum[0]
 
-    def homes(o, carry):
+    def homes(i, carry):
+        o = turn(i)
         for a in outward(o):
             src = a[0]
-            where = lax.rem(me + o, count)
+            where = ahead(o)
             dst = (
                 text_out.at[0, :, columns(where)]
                 if src.shape[0] == text
@@ -502,6 +519,8 @@
         partial += finish(
             into[:, j * tile : (j + 1) * tile].astype(jnp.float32), other * half + j * tile, tile
         )
+    leave = pltpu.make_async_copy(velocity, velocity_out, lsem.at[4])
+    leave.start()
     terms[0] = jnp.broadcast_to(partial, terms.shape[1:])
 
     def tell(o):
@@ -526,6 +545,7 @@
     lax.fori_loop(1, count, drain, 0)
     for o in range(1, total):
         tell(o).wait()
+    leave.wait()
     whole = jnp.sum(jnp.sum(terms[...], axis=0)[0:1])
     loss[0] = whole / (image * velocity.shape[2] * total)
 
@@ -575,8 +595,9 @@
             jax.ShapeDtypeStruct((1,), jnp.float32),
         ),
         in_specs=[ANY] * 10 + [VMEM] * 5 + [smem] * 2,
-        out_specs=(VMEM, VMEM, smem),
-        scratch_shapes=[pltpu.VMEM((count * rows, wide), bf16)] * 4
+        out_specs=(ANY, VMEM, smem),
+        scratch_shapes=[pltpu.VMEM((1, image, width), bf16)]
+        + [pltpu.VMEM((count * rows, wide), bf16)] * 4
         + [
             pltpu.VMEM((cores * image, attn), bf16),
             pltpu.VMEM((attn, half), bf16),
@@ -591,7 +612,7 @@
             dma((count,)), dma((count,)),
             dma((2, seq)), dma((2, seq)), dma((2, 2, seq)), dma((2, 2, seq)),
             dma((2, 2, seq)), dma((2, 2, seq)),
-            dma((4,)), dma((half // tile,)), dma((half // tile,)), dma((total,)), dma((total,)),
+            dma((5,)), dma((half // tile,)), dma((half // tile,)), dma((total,)), dma((total,)),
         ],
         compiler_params=pltpu.CompilerParams(
             collective_id=0, has_side_effects=True, vmem_limit_bytes=60 * 2**20

time: 105 us -> 104 us (level)
  no operation moved by 1% of the time
where the time goes in v3:
time: 104 us
  Pallas kernels  97.7 us (94%)
  between operations  3.63 us (3%)
  local copies, waits for them, and re-layouts  2.73 us (3%)
    pallas_call x1, Pallas kernels, fast(): pl.pallas_call(functools.partial(whole_kernel, sizes, dim ** (-0.5), tile...  97.7 us
    unnamed x4, local copies, waits for them, and re-layouts  2.73 us

profile of v3, /device:TPU:0, one launch (start us, length us, event | category | flops | bytes accessed | tf_op | source)
XLA Modules:
  0.0 104.1 jit_solution(304666201996684964)
XLA Ops:
  1.9 97.7 %shard_map.184 = (bf16[1,128,3072]{2,1,0:T(8,128)(2,1)}, bf16[1,16,2048]{2,1,0:T(8,128)(2,1)}, f32[1]{0:T(128)}) custom-call(bf16[1,16,2048]{2,1,0:T(8,128)(2,1)} %qt.1, bf16[1,128,2048]{2,1,0:T(8,128)(2,1)} %qi.1, bf16[1,16,2048]{2,1,0:T(8,128)(2,1)} %kt.1, bf16[1,128,2048]{2,1,0:T(8,128)(2,1)} %ki.1, bf16[1,16,2048]{2,1,0:T(8,128)(2,1)} %vt.1, ...), custom_call_target="tpu_custom_call" | custom-call | tf_op jit(solution)/shard_map/pallas_call | solution.py:590
  99.7 0.0 copy-start
  99.7 2.1 %copy.25 = bf16[1,128,3072]{2,1,0:T(8,128)(2,1)} copy(bf16[1,128,3072]{2,1,0:T(8,128)(2,1)} %get-tuple-element.6) | data formatting | bytes 1572864
  101.8 0.0 copy-done
  101.8 0.6 copy.26
Async XLA Ops:
  99.7 2.1 %copy-start = (bf16[1,16,2048]{2,1,0:T(8,128)(2,1)S(1)}, bf16[1,16,2048]{2,1,0:T(8,128)(2,1)}, u32[]{:S(2)}) copy-start(bf16[1,16,2048]{2,1,0:T(8,128)(2,1)} %get-tuple-element.7) | copy-start | bytes 196612
